TPU v7x, 256 devices: a whole 4x4x8 slice. The times are simulated.
256 devices in a mesh: gz: 8 (over x, y_hi), xy: 32 (over z, y_lo, core).
Axes of the slice: x: 4, y: 4 (y_hi: 2, y_lo: 2; y = y_hi * 2 + y_lo), z: 8, core: 2. Of those that a mesh axis runs over, the one named last changes fastest.
Arguments:
- positions: float32 [3, 8, 32, 128], P(None, 'gz', 'xy'), may hold values from 0 to 1
- features: bfloat16 [128, 8, 32, 128], P(None, 'gz', 'xy'), may hold values from -6 to 6
- cell_counts: int32 [8, 32], P('gz', 'xy'), may hold values from 32 to 128, as said below
- radial_weights: float32 [8, 128], replicated, may hold values from -0.75 to 0.75
- mix_weights: bfloat16 [128, 128], replicated, may hold values from -0.5 to 0.5
- out_weights: float32 [128], replicated, may hold values from -0.6 to 0.6
- charge_weights: float32 [128], replicated, may hold values from -0.5 to 0.5
- spline_base: int32 [3, 8, 32, 128], P(None, 'gz', 'xy'), may hold values from 0 to 255, as said below
- spline_weights: float32 [3, 4, 8, 32, 128], P(None, None, 'gz', 'xy'), may hold values from 0 to 0.5
- spline_slopes: float32 [3, 4, 8, 32, 128], P(None, None, 'gz', 'xy'), may hold values from -2.25 to 2.25, as said below
Outputs:
- energy_atom: float32 [8, 32, 128], P('gz', 'xy')
- forces: float32 [3, 8, 32, 128], P(None, 'gz', 'xy')
Inputs may be any that keep to these rules, and one draw needn't show every extreme that they name: Slots 0 to cell_counts - 1 of a cell hold atoms and the other slots are padding; some cell holds 128 atoms. For an atom of cell (cz, cx), spline_base[0] lies in cz * 16 to (cz + 1) * 16 - 1 and spline_base[1] in cx * 8 to (cx + 1) * 8 - 1; spline_base[2] lies in 0 to 255. `spline_slopes`: for each atom and each dimension the four slopes sum to zero.
All inputs are finite; a program needn't handle non-finite values.
Results may differ from a plain program's by a relative error of at most 0.003.
Values sent between devices are 32-bit elements; how exact they have to be, the bound alone decides.
A program may use at most 128 MiB of HBM per device.

v0:
```python
import functools

import jax
import jax.numpy as jnp
import numpy as np
from jax import lax
from jax.experimental import pallas as pl
from jax.experimental.pallas import tpu as pltpu
from jax.sharding import PartitionSpec as P

MESH = pl.DeviceIdType.MESH
F32 = jnp.float32
BF16 = jnp.bfloat16

K = 8
F = 128
T = 128
BZ = 16
BX = 8
EZ = BZ + 3
EX = BX + 3
ABP = 256
EDGE_LEN = 6.0
PERIOD_Y = 36.0
CUTOFF = 6.0
SOFTEN = 0.04
EWALD_BETA = 8.0
COULOMB = 4.0
JC = 32
OFFSETS = [(dz, dx) for dz in (-1, 0, 1) for dx in (-1, 0, 1)]
PAY = 136


def split_np(x):
    x = np.asarray(x, np.float32)
    hi = x.astype(jnp.bfloat16)
    lo = (x - hi.astype(np.float32)).astype(jnp.bfloat16)
    return np.stack([hi, lo])


@functools.lru_cache(None)
def tables(G, S):
    MZ, MX, MY, N = G * BZ, S * BX, G * S, G * S
    p = np.arange(MY)
    ky = np.where(p <= MY // 2, p, p - MY // 2)
    ang = 2 * np.pi * ((ky[:, None] * np.arange(MY)[None, :]) % MY) / MY
    ct = np.where((p <= MY // 2)[:, None], np.cos(ang), np.sin(ang))
    kzl = np.repeat(np.arange(G), S)
    kxl = np.tile(np.arange(S), G)
    ang = 2 * np.pi * (((kzl[:, None] * kzl[None, :]) % G) / G + ((kxl[:, None] * kxl[None, :]) % S) / S)
    w = np.concatenate([np.cos(ang), -np.sin(ang)], axis=0)
    a = np.repeat(np.arange(EZ), EX)
    b = np.tile(np.arange(EX), EZ)
    ang = 2 * np.pi * (kzl[:, None] * (a - 1)[None] / MZ + kxl[:, None] * (b - 1)[None] / MX)
    pad = ((0, 0), (0, ABP - EZ * EX))
    tw = np.stack([np.pad(np.cos(ang), pad), np.pad(-np.sin(ang), pad)]).astype(np.float32)
    kzh = np.repeat(np.arange(BZ), BX)
    kxh = np.tile(np.arange(BX), BZ)
    ang = 2 * np.pi * ((a - 1)[:, None] * kzh[None] / BZ + (b - 1)[:, None] * kxh[None] / BX)
    pad = ((0, ABP - EZ * EX), (0, 0))
    mr, mi = np.pad(np.cos(ang), pad), np.pad(-np.sin(ang), pad)
    fm = np.block([[mr, mi], [-mi, mr]])
    return split_np(ct), split_np(w), tw, split_np(fm)


def fit(fn, degree, top):
    z = top * (0.5 - 0.5 * np.cos(np.pi * (np.arange(200) + 0.5) / 200))
    return [float(c) for c in np.polynomial.polynomial.polyfit(z, fn(z), degree)]


COS_C = fit(lambda z: np.cos(np.pi * np.sqrt(z)), 6, 0.2526)
SIN_C = fit(lambda z: np.sin(np.pi * np.sqrt(z + 1e-300)) / np.sqrt(z + 1e-300), 5, 0.2526)


def poly(coefs, z):
    acc = jnp.full_like(z, coefs[-1])
    for c in coefs[-2::-1]:
        acc = acc * z + c
    return acc


def split(x):
    hi = x.astype(BF16)
    return hi, (x - hi.astype(F32)).astype(BF16)


def dg(a, b, dims):
    return lax.dot_general(a, b, (dims, ((), ())), preferred_element_type=F32)


NN = ((1,), (0,))
NT = ((1,), (1,))
TN = ((0,), (0,))


def dot3(a, b, dims):
    return dg(a[0], b[0], dims) + (dg(a[0], b[1], dims) + dg(a[1], b[0], dims))


def columns(row_block):
    return jnp.transpose(row_block)


def geometry(own, near, off_z, off_x, keep):
    dz = (off_z + near[0] - own[0]) * EDGE_LEN
    dx = (off_x + near[1] - own[1]) * EDGE_LEN
    dy = near[2] - own[2]
    dy = jnp.where(dy > 0.5, dy - 1.0, jnp.where(dy < -0.5, dy + 1.0, dy)) * PERIOD_Y
    rsq = dz * dz + dx * dx + dy * dy
    r2 = rsq + SOFTEN
    rinv = lax.rsqrt(r2)
    r = r2 * rinv
    x = jnp.minimum(r, 6.014) * (1.0 / CUTOFF) - 0.5
    z = x * x
    s1 = poly(COS_C, z)
    c1 = -x * poly(SIN_C, z)
    m = jnp.maximum(1.0 - rsq * (1.0 / (CUTOFF * CUTOFF)), 0.0)
    if keep is not None:
        m = m * keep
    env = m * m
    u = (dz * rinv, dx * rinv, dy * rinv)
    return rinv, s1, c1, m, env, u


def kernel(
    G, S,
    pos_ref, feat_ref, cnt_ref, rw_ref, mix_ref, ow_ref, cw_ref, base_ref, wts_ref, slp_ref,
    ct_hbm, w_hbm, tw_hbm, fm_hbm,
    e_out, f_out,
    ct, w, tw, fm, halo, rwb, post, pv, radf, msg, gm, gp, nf, ff, fr,
    ee, wzx, spec, plane, back, field,
    tab_sem, hs, hr, fs, fr_sem, as_, ar, bs, br, ls, phase, halo_t,
):
    N = G * S
    MY = N
    g = lax.axis_index("gz")
    s = lax.axis_index("xy")
    me = g * S + s

    def peer(dz, dx):
        return (lax.rem(g + (dz + G), G), lax.rem(s + (dx + S), S))

    bar = pltpu.get_barrier_semaphore()
    diag = [(dz, dx) for dz in (-1, 1) for dx in (-1, 1)]
    for dz, dx in diag:
        pl.semaphore_signal(bar, inc=1, device_id=peer(dz, dx), device_id_type=MESH)
    for dz in range(1, G):
        pl.semaphore_signal(bar, inc=1, device_id=peer(dz, 0), device_id_type=MESH)

    def sig_row(k, _):
        pl.semaphore_signal(bar, inc=1, device_id=(g, lax.rem(s + k, S)), device_id_type=MESH)
        return 0

    lax.fori_loop(1, S, sig_row, 0)

    tabs = [pltpu.make_async_copy(h, v, tab_sem.at[i]) for i, (h, v) in enumerate(
        [(ct_hbm, ct), (w_hbm, w), (tw_hbm, tw), (fm_hbm, fm)])]
    for t in tabs:
        t.start()

    lane = lax.broadcasted_iota(jnp.int32, (1, T), 1)
    valid = (lane < cnt_ref[0, 0]).astype(F32)
    featv = feat_ref[...].astype(F32) * valid
    halo[4, 0:F, :] = featv
    halo[4, F:F + 8, :] = jnp.concatenate([pos_ref[...], jnp.zeros((5, T), F32)], axis=0)
    cwt = columns(jnp.broadcast_to(cw_ref[...], (8, F)))
    owt = columns(jnp.broadcast_to(ow_ref[...], (8, F)))
    charge = jnp.sum(featv * cwt[:, 0:1], axis=0, keepdims=True)

    yrow = lax.broadcasted_iota(jnp.int32, (MY, T), 0)
    ty = jnp.bitwise_and(yrow - base_ref[2:3, :] + 1, MY - 1)
    wy = jnp.zeros((MY, T), F32)
    sy = jnp.zeros((MY, T), F32)
    for c in range(4):
        hit = ty == c
        wy = wy + jnp.where(hit, wts_ref[8 + c:9 + c, :], 0.0)
        sy = sy + jnp.where(hit, slp_ref[8 + c:9 + c, :], 0.0)
    ab = lax.broadcasted_iota(jnp.int32, (ABP, T), 0)
    arow = lax.shift_right_logical(ab * 373, 12)
    brow = ab - arow * EX
    tz = arow - (base_ref[0:1, :] - g * BZ)
    tx = brow - (base_ref[1:2, :] - s * BX)
    zero = jnp.zeros((ABP, T), F32)
    wz, sz, wx, sx = zero, zero, zero, zero
    for c in range(4):
        hit = tz == c
        wz = wz + jnp.where(hit, wts_ref[c:c + 1, :], 0.0)
        sz = sz + jnp.where(hit, slp_ref[c:c + 1, :], 0.0)
        hit = tx == c
        wx = wx + jnp.where(hit, wts_ref[4 + c:5 + c, :], 0.0)
        sx = sx + jnp.where(hit, slp_ref[4 + c:5 + c, :], 0.0)
    wzx[0] = wz * wx
    wzx[1] = sz * wx
    wzx[2] = wz * sx

    tabs[0].wait()
    yw = split(jnp.concatenate([wy, sy], axis=1))
    e_all = dot3((ct[0], ct[1]), yw, NN)
    eh, el = split(e_all)
    ee[0] = eh
    ee[1] = el
    spectrum = dot3((eh[:, :T], el[:, :T]), split(wzx[0] * charge), NT)
    spec[:, 0, :] = spectrum[:, :128]
    spec[:, 1, :] = spectrum[:, 128:]

    pl.semaphore_wait(bar, 4 + G - 1 + S - 1)

    def sig_phase(k, _):
        pl.semaphore_signal(phase, inc=1, device_id=(g, lax.rem(s + k, S)), device_id_type=MESH)
        return 0

    lax.fori_loop(1, S, sig_phase, 0)

    halo_copies = []
    for n, (dz, dx) in enumerate(OFFSETS):
        if n == 4:
            continue
        cp = pltpu.make_async_remote_copy(
            src_ref=halo.at[4], dst_ref=halo.at[8 - n], send_sem=hs.at[n], recv_sem=hr.at[8 - n],
            device_id=peer(dz, dx), device_id_type=MESH)
        cp.start()
        halo_copies.append(cp)

    pl.semaphore_wait(phase, S - 1)

    def exchange(src, dst, send_sem, recv_sem):
        own = pltpu.make_async_copy(src.at[me], dst.at[me], ls)
        own.start()

        def send(k, _):
            q = lax.rem(me + k, N)
            pltpu.make_async_remote_copy(
                src_ref=src.at[q], dst_ref=dst.at[me], send_sem=send_sem, recv_sem=recv_sem,
                device_id=(q // S, lax.rem(q, S)), device_id_type=MESH).start()
            return 0

        lax.fori_loop(1, N, send, 0)
        own.wait()

    def arrived(dst, sem):
        pltpu.make_async_copy(dst.at[pl.ds(0, N - 1)], dst.at[pl.ds(0, N - 1)], sem).wait()

    exchange(spec, plane, as_, ar)

    rwt = columns(rw_ref[...])
    for k in range(K):
        rwb[k] = jnp.broadcast_to(rwt[:, k:k + 1], (F, T))
    msg[...] = jnp.zeros_like(msg)
    for cp in halo_copies:
        cp.wait_recv()
    own_rows = [pos_ref[c:c + 1, :] for c in range(3)]
    lane_c = lax.broadcasted_iota(jnp.int32, (JC, T), 1)
    row_c = lax.broadcasted_iota(jnp.int32, (JC, T), 0)

    def pair_inputs(n, j0):
        near = [jnp.broadcast_to(post[n, pl.ds(j0, JC), c:c + 1], (JC, T)) for c in range(3)]
        off_z = (n // 3 - 1).astype(F32)
        off_x = (lax.rem(n, 3) - 1).astype(F32)
        same = jnp.logical_and(row_c + j0 == lane_c, n == 4)
        keep = jnp.where(same, 0.0, 1.0)
        return geometry(own_rows, near, off_z, off_x, keep)

    def forward(n, _):
        post[n] = jnp.transpose(halo[n, F:F + 8, :])
        feat = halo[n, 0:F, :]
        for k in range(K):
            radf[:, k * T:(k + 1) * T] = (feat * rwb[k]).astype(BF16)

        def chunk(t, _):
            j0 = pl.multiple_of(t * JC, JC)
            rinv, s1, c1, m, env, u = pair_inputs(n, j0)
            amp = env * rinv
            two_c = 2.0 * c1
            s_prev, s_now = jnp.zeros_like(s1), s1
            for k in range(K):
                e = s_now * amp
                rows = pl.ds(k * T + j0, JC)
                pv[rows, 0:T] = e.astype(BF16)
                for c in range(3):
                    pv[rows, (c + 1) * T:(c + 2) * T] = (e * u[c]).astype(BF16)
                s_prev, s_now = s_now, two_c * s_now - s_prev
            return 0

        lax.fori_loop(0, T // JC, chunk, 0)
        msg[...] += dg(radf[...], pv[...], NN)
        return 0

    lax.fori_loop(0, 9, forward, 0)

    m0 = msg[:, 0:T]
    mc = [msg[:, (c + 1) * T:(c + 2) * T] for c in range(3)]
    inv = (m0 + (mc[0] * mc[0] + mc[1] * mc[1] + mc[2] * mc[2])).astype(BF16)
    mix = mix_ref[...]
    pre = dg(mix, inv, TN)
    sig = 1.0 / (1.0 + jnp.exp(-pre))
    owc = owt[:, 0:1]
    energy_sr = jnp.sum(pre * sig * owc, axis=0, keepdims=True)
    grad_pre = ((sig + pre * sig * (1.0 - sig)) * owc * valid).astype(BF16)
    grad_inv = dg(mix, grad_pre, NN)
    gm[:, 0:T] = grad_inv.astype(BF16)
    for c in range(3):
        gm[:, (c + 1) * T:(c + 2) * T] = (2.0 * mc[c] * grad_inv).astype(BF16)

    for t in tabs[1:]:
        t.wait()
    arrived(plane, ar)
    rs = split(jnp.concatenate([plane[:, 0, :], plane[:, 1, :]], axis=1))
    yr = dot3((w[0, 0:N], w[1, 0:N]), rs, NN)
    yi = dot3((w[0, N:], w[1, N:]), rs, NN)
    tr, ti = tw[0], tw[1]
    yy = split(jnp.concatenate([tr * yr - ti * yi, tr * yi + ti * yr], axis=1))
    zz = dot3(yy, (fm[0], fm[1]), NN)
    kk = lax.broadcasted_iota(jnp.int32, (N, 128), 0)
    hh = lax.broadcasted_iota(jnp.int32, (N, 128), 1)
    kz = kk // S + G * (hh // BX)
    kx = lax.rem(kk, S) + S * lax.rem(hh, BX)
    mz_, mx_ = G * BZ, S * BX
    kz = (kz - mz_ * (2 * kz >= mz_).astype(jnp.int32)).astype(F32)
    kx = (kx - mx_ * (2 * kx >= mx_).astype(jnp.int32)).astype(F32)
    ky_i = jnp.where(me <= MY // 2, me, me - MY // 2)
    ky = ky_i.astype(F32)
    twice = jnp.where(jnp.logical_or(me == 0, me == MY // 2), 1.0, 2.0)
    len_z, len_x = EDGE_LEN * G, EDGE_LEN * S
    fz, fx, fy = kz * (1.0 / len_z), kx * (1.0 / len_x), ky * (1.0 / PERIOD_Y)
    wsq = fz * fz + fx * fx + fy * fy
    positive = wsq > 0
    safe = jnp.where(positive, wsq, 1.0)
    green = COULOMB * jnp.exp(safe * (-np.pi ** 2 / EWALD_BETA ** 2)) / (
        np.pi * len_z * len_x * PERIOD_Y * safe)
    green = jnp.where(positive, green * twice, 0.0)
    zs = split(zz * jnp.concatenate([green, green], axis=1))
    vv = dot3(zs, (fm[0], fm[1]), NT)
    vr, vi = vv[:, :ABP], vv[:, ABP:]
    pr = split(tr * vr + ti * vi)
    pi_ = split(tr * vi - ti * vr)
    uu = dot3((w[0, 0:N], w[1, 0:N]), pr, NN) + dot3((w[0, N:], w[1, N:]), pi_, NN)
    back[:, 0, :] = uu[:, :128]
    back[:, 1, :] = uu[:, 128:]

    exchange(back, field, bs, br)

    def backward(n, own):
        feat_t = jnp.transpose(halo[n, 0:F, :])
        halo_t[...] = feat_t

        def chunk(t, own):
            j0 = pl.multiple_of(t * JC, JC)
            ft = halo_t[pl.ds(j0, JC), :]
            rad_t = jnp.concatenate([(ft * rw_ref[k:k + 1, :]).astype(BF16) for k in range(K)], axis=0)
            gp[...] = dg(rad_t, gm[...], NN)
            rinv, s1, c1, m, env, u = pair_inputs(n, j0)
            amp = env * rinv
            damp = -(m * (1.0 / 9.0) + env * (rinv * rinv))
            two_c = 2.0 * c1
            s_prev, s_now = jnp.zeros_like(s1), s1
            c_prev, c_now = jnp.ones_like(c1), c1
            sums = [None] * 4
            kcs = [None] * 4
            for k in range(K):
                kc = c_now * float(k + 1)
                for c in range(4):
                    v = gp[k * JC:(k + 1) * JC, c * T:(c + 1) * T]
                    sums[c] = v * s_now if k == 0 else sums[c] + v * s_now
                    kcs[c] = v * kc if k == 0 else kcs[c] + v * kc
                s_prev, s_now = s_now, two_c * s_now - s_prev
                c_prev, c_now = c_now, two_c * c_now - c_prev
            ar_ = amp * rinv
            tc = [ar_ * sums[c + 1] for c in range(3)]
            s_q = sums[0] + (u[0] * sums[1] + u[1] * sums[2] + u[2] * sums[3])
            k_q = kcs[0] + (u[0] * kcs[1] + u[1] * kcs[2] + u[2] * kcs[3])
            br_ = (amp * (np.pi / CUTOFF)) * k_q + damp * s_q - (u[0] * tc[0] + u[1] * tc[1] + u[2] * tc[2])
            grads = [tc[c] + u[c] * br_ for c in range(3)]
            for c in range(3):
                nf[n, pl.ds(j0, JC), c:c + 1] = -jnp.sum(grads[c], axis=1, keepdims=True)
            return tuple(
                own[c] + sum(grads[c][i * 8:(i + 1) * 8] for i in range(JC // 8)) for c in range(3))

        own = lax.fori_loop(0, T // JC, chunk, own)
        ff[n] = jnp.transpose(nf[n])[0:8, :]
        return own

    zero8 = jnp.zeros((8, T), F32)
    nf[...] = jnp.zeros_like(nf)
    own = lax.fori_loop(0, 9, backward, (zero8, zero8, zero8))

    force_copies = []
    for n, (dz, dx) in enumerate(OFFSETS):
        if n == 4:
            continue
        cp = pltpu.make_async_remote_copy(
            src_ref=ff.at[n], dst_ref=fr.at[8 - n], send_sem=fs.at[n], recv_sem=fr_sem.at[8 - n],
            device_id=peer(dz, dx), device_id_type=MESH)
        cp.start()
        force_copies.append(cp)

    arrived(field, br)
    phi = split(jnp.concatenate([field[:, 0, :], field[:, 1, :]], axis=1))
    along = dot3(phi, (ee[0], ee[1]), TN)
    a_w, a_s = along[:, :T], along[:, T:]
    pot = jnp.sum(a_w * wzx[0], axis=0, keepdims=True)
    rec = [
        -charge * jnp.sum(a_w * wzx[1], axis=0, keepdims=True),
        -charge * jnp.sum(a_w * wzx[2], axis=0, keepdims=True),
        -charge * jnp.sum(a_s * wzx[0], axis=0, keepdims=True),
    ]
    e_out[...] = valid * (energy_sr + 0.5 * charge * pot)

    for cp in force_copies:
        cp.wait_recv()
    near = ff[4]
    for n in range(9):
        if n != 4:
            near = near + fr[n]
    for c in range(3):
        f_out[c:c + 1, :] = jnp.sum(own[c], axis=0, keepdims=True) + near[c:c + 1, :] + rec[c]

    for cp in halo_copies + force_copies:
        cp.wait_send()
    arrived(spec, as_)
    arrived(back, bs)


def local(G, S, positions, features, cell_counts, radial_weights, mix_weights, out_weights,
          charge_weights, spline_base, spline_weights, spline_slopes):
    N = G * S
    vm = pl.BlockSpec(memory_space=pltpu.VMEM)
    anys = pl.BlockSpec(memory_space=pl.ANY)
    V = pltpu.VMEM
    DMA = pltpu.SemaphoreType.DMA
    e, f = pl.pallas_call(
        functools.partial(kernel, G, S),
        out_shape=(jax.ShapeDtypeStruct((1, T), F32), jax.ShapeDtypeStruct((3, T), F32)),
        in_specs=[vm, vm, pl.BlockSpec(memory_space=pltpu.SMEM)] + [vm] * 7 + [anys] * 4,
        out_specs=[vm, vm],
        scratch_shapes=[
            V((2, N, N), BF16), V((2, 2 * N, N), BF16), V((2, N, ABP), F32), V((2, 2 * ABP, 256), BF16),
            V((9, PAY, T), F32), V((K, F, T), F32), V((9, T, 8), F32), V((K * T, 4 * T), BF16),
            V((F, K * T), BF16), V((F, 4 * T), F32), V((F, 4 * T), BF16), V((K * JC, 4 * T), F32),
            V((9, T, 128), F32), V((9, 8, T), F32), V((9, 8, T), F32),
            V((2, N, 2 * T), BF16), V((3, ABP, T), F32),
            V((N, 2, 128), F32), V((N, 2, 128), F32), V((N, 2, 128), F32), V((N, 2, 128), F32),
            DMA((4,)), DMA((9,)), DMA((9,)), DMA((9,)), DMA((9,)),
            DMA, DMA, DMA, DMA, DMA, pltpu.SemaphoreType.REGULAR,
            V((T, F), F32),
        ],
        compiler_params=pltpu.CompilerParams(collective_id=0, has_side_effects=True,
                                             vmem_limit_bytes=40 * 1024 * 1024),
    )(
        positions.reshape(3, T), features.reshape(F, T), cell_counts, radial_weights, mix_weights,
        out_weights.reshape(1, F), charge_weights.reshape(1, F), spline_base.reshape(3, T),
        spline_weights.reshape(12, T), spline_slopes.reshape(12, T),
        *[jnp.asarray(t) for t in tables(G, S)],
    )
    return e.reshape(1, 1, T), f.reshape(3, 1, 1, T)


def solution(mesh):
    placed = (
        P(None, "gz", "xy", None), P(None, "gz", "xy", None), P("gz", "xy"), P(), P(), P(), P(),
        P(None, "gz", "xy", None), P(None, None, "gz", "xy", None), P(None, None, "gz", "xy", None),
    )
    return jax.shard_map(
        functools.partial(local, mesh.shape["gz"], mesh.shape["xy"]),
        mesh=mesh, in_specs=placed,
        out_specs=(P("gz", "xy", None), P(None, "gz", "xy", None)),
        check_vma=False,
    )
```

profile of v0, /device:TPU:1, one launch (start us, length us, event | category | flops | bytes accessed | tf_op | source)
XLA Modules:
  0.0 70.6 jit_solution(16462978389115153759)
XLA Ops:
  0.6 0.0 copy-start.9
  0.6 0.7 pad
  1.3 0.0 copy-start.10
  1.3 0.0 copy-start.11
  1.4 0.0 copy-start.5
  1.4 0.0 copy-start.4
  1.4 0.0 copy-done.9
  1.4 0.6 copy-done.10
  2.0 0.0 copy-done.11
  2.0 0.0 copy-start.6
  2.7 0.0 copy-start.7
  2.7 0.0 copy-start.8
  2.7 0.0 copy-done.5
  2.7 0.0 copy-done.4
  2.8 0.0 copy-done.6
  2.8 0.6 copy-done.7
  3.4 0.0 copy-done.8
  3.4 0.0 copy-start
  3.4 1.0 %copy-done = f32[2,256,256]{2,1,0:T(8,128)S(1)} copy-done((f32[2,256,256]{2,1,0:T(8,128)S(1)}, f32[2,256,256]{2,1,0:T(8,128)}, u32[]{:S(2)}) %copy-start) | copy-done | bytes 524312
  4.4 0.0 copy-start.1
  4.4 1.0 %copy-done.1 = bf16[2,512,256]{2,1,0:T(8,128)(2,1)S(1)} copy-done((bf16[2,512,256]{2,1,0:T(8,128)(2,1)S(1)}, bf16[2,512,256]{2,1,0:T(8,128)(2,1)}, u32[]{:S(2)}) %copy-start.1) | copy-done | bytes 524312
  5.5 0.0 copy-start.2
  5.5 1.0 %copy-done.2 = bf16[2,512,256]{2,1,0:T(8,128)(2,1)S(1)} copy-done((bf16[2,512,256]{2,1,0:T(8,128)(2,1)S(1)}, bf16[2,512,256]{2,1,0:T(8,128)(2,1)}, u32[]{:S(2)}) %copy-start.2) | copy-done | bytes 524312
  6.5 0.0 copy-start.3
  6.5 0.9 %copy-done.3 = bf16[2,256,256]{2,1,0:T(8,128)(2,1)S(1)} copy-done((bf16[2,256,256]{2,1,0:T(8,128)(2,1)S(1)}, bf16[2,256,256]{2,1,0:T(8,128)(2,1)}, u32[]{:S(2)}) %copy-start.3) | copy-done | bytes 262168
  7.5 62.1 %shard_map.149 = (f32[1,128]{1,0:T(1,128)S(1)}, f32[3,128]{1,0:T(4,128)S(1)}) custom-call(f32[3,128]{1,0:T(4,128)S(1)} %bitcast.25, bf16[128,128]{1,0:T(8,128)(2,1)S(1)} %bitcast.21, s32[1,1]{1,0:T(1,128)S(6)} %copy.32.cnt_ref, f32[8,128]{1,0:T(8,128)S(1)} %copy-done.6, bf16[128,128]{1,0:T(8,128)(2,1)S(1)} %copy-done.5, f32[1,128]{1,0:T(1,128)S(1)} %bitcast.27, ...), custom_call_target="tpu_custom_call" | custom-call | tf_op jit(solution)/shard_map/pallas_call | solution.py:430
  69.6 0.6 copy.16
  70.1 0.5 copy.33
  (5 shorter events, 0.0 us)
Async XLA Ops:
  0.6 0.8 %copy-start.9 = (f32[3,4,1,1,128]{4,3,2,1,0:T(1,128)S(1)}, f32[3,4,1,1,128]{4,3,2,1,0:T(1,128)}, u32[]{:S(2)}) copy-start(f32[3,4,1,1,128]{4,3,2,1,0:T(1,128)} %param.23) | copy-start | bytes 18436
  1.3 0.7 copy-start.10
  1.3 0.7 copy-start.11
  1.4 1.4 %copy-start.5 = (bf16[128,128]{1,0:T(8,128)(2,1)S(1)}, bf16[128,128]{1,0:T(8,128)(2,1)}, u32[]{:S(2)}) copy-start(bf16[128,128]{1,0:T(8,128)(2,1)} %mix_ref.1) | copy-start | bytes 98308
  1.4 1.4 %copy-start.4 = (bf16[128,1,1,128]{3,0,2,1:T(8,128)(2,1)S(1)}, bf16[128,1,1,128]{3,0,2,1:T(8,128)(2,1)}, u32[]{:S(2)}) copy-start(bf16[128,1,1,128]{3,0,2,1:T(8,128)(2,1)} %param.15) | copy-start | bytes 98308
  2.0 0.7 %copy-start.6 = (f32[8,128]{1,0:T(8,128)S(1)}, f32[8,128]{1,0:T(8,128)}, u32[]{:S(2)}) copy-start(f32[8,128]{1,0:T(8,128)} %rw_ref.1) | copy-start | bytes 12292
  2.7 0.7 copy-start.7
  2.7 0.7 copy-start.8
  3.4 1.0 %copy-start = (f32[2,256,256]{2,1,0:T(8,128)S(1)}, f32[2,256,256]{2,1,0:T(8,128)}, u32[]{:S(2)}) copy-start(f32[2,256,256]{2,1,0:T(8,128)} %constant.10.clone.tw_hbm) | copy-start | bytes 1572868
  4.4 1.0 %copy-start.1 = (bf16[2,512,256]{2,1,0:T(8,128)(2,1)S(1)}, bf16[2,512,256]{2,1,0:T(8,128)(2,1)}, u32[]{:S(2)}) copy-start(bf16[2,512,256]{2,1,0:T(8,128)(2,1)} %constant.11.clone.fm_hbm) | copy-start | bytes 1572868
  5.5 1.0 %copy-start.2 = (bf16[2,512,256]{2,1,0:T(8,128)(2,1)S(1)}, bf16[2,512,256]{2,1,0:T(8,128)(2,1)}, u32[]{:S(2)}) copy-start(bf16[2,512,256]{2,1,0:T(8,128)(2,1)} %constant.9.clone.w_hbm) | copy-start | bytes 1572868
  6.5 0.9 %copy-start.3 = (bf16[2,256,256]{2,1,0:T(8,128)(2,1)S(1)}, bf16[2,256,256]{2,1,0:T(8,128)(2,1)}, u32[]{:S(2)}) copy-start(bf16[2,256,256]{2,1,0:T(8,128)(2,1)} %constant.8.clone.ct_hbm) | copy-start | bytes 786436
where the time goes:
time: 71 us; the launch traced here: 70.6 us
  Pallas kernels  62.1 us (87%)
  local copies, waits for them, and re-layouts  7.13 us (10%)
  between operations  1.41 us (2%)
    pallas_call x1, Pallas kernels, local(): pl.pallas_call(functools.partial(kernel, G, S), out_shape=(jax.ShapeDtype...  62.1 us
    unnamed x32, local copies, waits for them, and re-layouts  7.13 us

commit v1 on v0

v1 whole, which is shorter than its diff:
```python
import functools

import jax
import jax.numpy as jnp
import numpy as np
from jax import lax
from jax.experimental import pallas as pl
from jax.experimental.pallas import tpu as pltpu
from jax.sharding import PartitionSpec as P

MESH = pl.DeviceIdType.MESH
F32 = jnp.float32
BF16 = jnp.bfloat16

K = 8
F = 128
T = 128
BZ = 16
BX = 8
EZ = BZ + 3
EX = BX + 3
ABP = 256
EDGE_LEN = 6.0
PERIOD_Y = 36.0
CUTOFF = 6.0
SOFTEN = 0.04
EWALD_BETA = 8.0
COULOMB = 4.0
IC = 32
OFFSETS = [(dz, dx) for dz in (-1, 0, 1) for dx in (-1, 0, 1)]


def split_np(x):
    x = np.asarray(x, np.float32)
    hi = x.astype(jnp.bfloat16)
    lo = (x - hi.astype(np.float32)).astype(jnp.bfloat16)
    return np.stack([hi, lo])


@functools.lru_cache(None)
def tables(G, S):
    MZ, MX, MY, N = G * BZ, S * BX, G * S, G * S
    p = np.arange(MY)
    ky = np.where(p <= MY // 2, p, p - MY // 2)
    ang = 2 * np.pi * ((ky[:, None] * np.arange(MY)[None, :]) % MY) / MY
    ct = np.where((p <= MY // 2)[:, None], np.cos(ang), np.sin(ang))
    kzl = np.repeat(np.arange(G), S)
    kxl = np.tile(np.arange(S), G)
    ang = 2 * np.pi * (((kzl[:, None] * kzl[None, :]) % G) / G + ((kxl[:, None] * kxl[None, :]) % S) / S)
    w = np.concatenate([np.cos(ang), -np.sin(ang)], axis=0)
    a = np.repeat(np.arange(EZ), EX)
    b = np.tile(np.arange(EX), EZ)
    ang = 2 * np.pi * (kzl[:, None] * (a - 1)[None] / MZ + kxl[:, None] * (b - 1)[None] / MX)
    pad = ((0, 0), (0, ABP - EZ * EX))
    tw = np.stack([np.pad(np.cos(ang), pad), np.pad(-np.sin(ang), pad)]).astype(np.float32)
    kzh = np.repeat(np.arange(BZ), BX)
    kxh = np.tile(np.arange(BX), BZ)
    ang = 2 * np.pi * ((a - 1)[:, None] * kzh[None] / BZ + (b - 1)[:, None] * kxh[None] / BX)
    pad = ((0, ABP - EZ * EX), (0, 0))
    mr, mi = np.pad(np.cos(ang), pad), np.pad(-np.sin(ang), pad)
    fm = np.block([[mr, mi], [-mi, mr]])
    return split_np(ct), split_np(w), tw, split_np(fm)


def fit(fn, degree, top):
    z = top * (0.5 - 0.5 * np.cos(np.pi * (np.arange(200) + 0.5) / 200))
    return [float(c) for c in np.polynomial.polynomial.polyfit(z, fn(z), degree)]


COS_C = fit(lambda z: np.cos(np.pi * np.sqrt(z)), 6, 0.2526)
SIN_C = fit(lambda z: np.sin(np.pi * np.sqrt(z + 1e-300)) / np.sqrt(z + 1e-300), 5, 0.2526)


def poly(coefs, z):
    acc = jnp.full_like(z, coefs[-1])
    for c in coefs[-2::-1]:
        acc = acc * z + c
    return acc


def split(x):
    hi = x.astype(BF16)
    return hi, (x - hi.astype(F32)).astype(BF16)


def dg(a, b, dims):
    return lax.dot_general(a, b, (dims, ((), ())), preferred_element_type=F32)


NN = ((1,), (0,))
NT = ((1,), (1,))
TN = ((0,), (0,))


def dot3(a, b, dims):
    return dg(a[0], b[0], dims) + (dg(a[0], b[1], dims) + dg(a[1], b[0], dims))


def geometry(own, near, off_z, off_x, keep):
    dz = (off_z + near[0] - own[0]) * EDGE_LEN
    dx = (off_x + near[1] - own[1]) * EDGE_LEN
    dy = near[2] - own[2]
    dy = jnp.where(dy > 0.5, dy - 1.0, jnp.where(dy < -0.5, dy + 1.0, dy)) * PERIOD_Y
    rsq = dz * dz + dx * dx + dy * dy
    r2 = rsq + SOFTEN
    rinv = lax.rsqrt(r2)
    r = r2 * rinv
    x = jnp.minimum(r, 6.014) * (1.0 / CUTOFF) - 0.5
    z = x * x
    s1 = poly(COS_C, z)
    c1 = -x * poly(SIN_C, z)
    m = jnp.maximum(1.0 - rsq * (1.0 / (CUTOFF * CUTOFF)), 0.0) * keep
    env = m * m
    u = (dz * rinv, dx * rinv, dy * rinv)
    return rinv, s1, c1, m, env, u


def kernel(
    G, S,
    pos_hbm, feat_hbm, cnt_hbm, rw_hbm, mix_hbm, ow_hbm, cw_hbm, base_hbm, wts_hbm, slp_hbm,
    ct_hbm, w_hbm, tw_hbm, fm_hbm,
    e_out, f_out,
    pos_ref, feat_ref, cnt_ref, rw_ref, mix_ref, ow_ref, cw_ref, base_ref, wts_ref, slp_ref,
    ct, w, tw, fm,
    halo, hpos, posb, pv, wk, dk, uu_, radt, msg, gm, gp_a, gp_b, own_acc, ff, fr,
    ee, wzx, spec, plane, back, field, grn,
    in_sem, hs, hr, ps, pr_, fs, fr_sem, as_, ar, bs, br, ls, phase,
):
    N = G * S
    MY = N
    g = lax.axis_index("gz")
    s = lax.axis_index("xy")
    me = g * S + s

    def peer(dz, dx):
        return (lax.rem(g + (dz + G), G), lax.rem(s + (dx + S), S))

    loads = [pltpu.make_async_copy(h, v, in_sem.at[i]) for i, (h, v) in enumerate([
        (feat_hbm, feat_ref), (cnt_hbm, cnt_ref), (cw_hbm, cw_ref), (base_hbm, base_ref),
        (wts_hbm, wts_ref), (slp_hbm, slp_ref), (pos_hbm, pos_ref), (ct_hbm, ct),
        (rw_hbm, rw_ref), (mix_hbm, mix_ref), (ow_hbm, ow_ref),
        (w_hbm, w), (tw_hbm, tw), (fm_hbm, fm)])]
    for t in loads:
        t.start()

    bar = pltpu.get_barrier_semaphore()
    diag = [(dz, dx) for dz in (-1, 1) for dx in (-1, 1)]
    for dz, dx in diag:
        pl.semaphore_signal(bar, inc=1, device_id=peer(dz, dx), device_id_type=MESH)
    for dz in range(1, G):
        pl.semaphore_signal(bar, inc=1, device_id=peer(dz, 0), device_id_type=MESH)

    def sig_row(k, _):
        pl.semaphore_signal(bar, inc=1, device_id=(g, lax.rem(s + k, S)), device_id_type=MESH)
        return 0

    lax.fori_loop(1, S, sig_row, 0)

    for t in loads[:8]:
        t.wait()
    lane = lax.broadcasted_iota(jnp.int32, (1, T), 1)
    valid = (lane < cnt_ref[...]).astype(F32)
    featv = feat_ref[...].astype(F32) * valid
    halo[4] = jnp.transpose(featv)
    hpos[4] = jnp.concatenate([pos_ref[c] for c in range(3)] + [jnp.zeros((5, T), F32)], axis=0)
    cwt = jnp.transpose(jnp.broadcast_to(cw_ref[...], (8, F)))
    charge = jnp.sum(featv * cwt[:, 0:1], axis=0, keepdims=True)

    yrow = lax.broadcasted_iota(jnp.int32, (MY, T), 0)
    ty = jnp.bitwise_and(yrow - base_ref[2] + 1, MY - 1)
    wy = jnp.zeros((MY, T), F32)
    sy = jnp.zeros((MY, T), F32)
    for c in range(4):
        hit = ty == c
        wy = wy + jnp.where(hit, wts_ref[8 + c], 0.0)
        sy = sy + jnp.where(hit, slp_ref[8 + c], 0.0)
    ab = lax.broadcasted_iota(jnp.int32, (ABP, T), 0)
    arow = lax.shift_right_logical(ab * 373, 12)
    brow = ab - arow * EX
    tz = arow - (base_ref[0] - g * BZ)
    tx = brow - (base_ref[1] - s * BX)
    zero = jnp.zeros((ABP, T), F32)
    wz, sz, wx, sx = zero, zero, zero, zero
    for c in range(4):
        hit = tz == c
        wz = wz + jnp.where(hit, wts_ref[c], 0.0)
        sz = sz + jnp.where(hit, slp_ref[c], 0.0)
        hit = tx == c
        wx = wx + jnp.where(hit, wts_ref[4 + c], 0.0)
        sx = sx + jnp.where(hit, slp_ref[4 + c], 0.0)
    wzx[0] = wz * wx
    wzx[1] = sz * wx
    wzx[2] = wz * sx

    yw = split(jnp.concatenate([wy, sy], axis=1))
    e_all = dot3((ct[0], ct[1]), yw, NN)
    eh, el = split(e_all)
    ee[0] = eh
    ee[1] = el
    spectrum = dot3((eh[:, :T], el[:, :T]), split(wzx[0] * charge), NT)
    spec[:, 0, :] = spectrum[:, :128]
    spec[:, 1, :] = spectrum[:, 128:]

    kk = lax.broadcasted_iota(jnp.int32, (N, 128), 0)
    hh = lax.broadcasted_iota(jnp.int32, (N, 128), 1)
    kz = kk // S + G * (hh // BX)
    kx = lax.rem(kk, S) + S * lax.rem(hh, BX)
    mz_, mx_ = G * BZ, S * BX
    kz = (kz - mz_ * (2 * kz >= mz_).astype(jnp.int32)).astype(F32)
    kx = (kx - mx_ * (2 * kx >= mx_).astype(jnp.int32)).astype(F32)
    ky = jnp.where(me <= MY // 2, me, me - MY // 2).astype(F32)
    twice = jnp.where(jnp.logical_or(me == 0, me == MY // 2), 1.0, 2.0)
    len_z, len_x = EDGE_LEN * G, EDGE_LEN * S
    fz, fx, fy = kz * (1.0 / len_z), kx * (1.0 / len_x), ky * (1.0 / PERIOD_Y)
    wsq = fz * fz + fx * fx + fy * fy
    positive = wsq > 0
    safe = jnp.where(positive, wsq, 1.0)
    green = COULOMB * jnp.exp(safe * (-np.pi ** 2 / EWALD_BETA ** 2)) / (
        np.pi * len_z * len_x * PERIOD_Y * safe)
    grn[...] = jnp.where(positive, green * twice, 0.0)

    own_t = jnp.transpose(hpos[4])
    for c in range(3):
        posb[c] = jnp.broadcast_to(own_t[:, c:c + 1], (T, T))

    lane_c = lax.broadcasted_iota(jnp.int32, (IC, T), 1)
    row_c = lax.broadcasted_iota(jnp.int32, (IC, T), 0)

    def pairs(n):
        off_z = (n // 3 - 1) * 1.0
        off_x = (lax.rem(n, 3) - 1) * 1.0
        near = [hpos[n, c:c + 1, :] for c in range(3)]

        def chunk(t, _):
            i0 = pl.multiple_of(t * IC, IC)
            rows = pl.ds(i0, IC)
            own = [posb[c, rows, :] for c in range(3)]
            same = jnp.logical_and(row_c + i0 == lane_c, n == 4)
            rinv, s1, c1, m, env, u = geometry(own, near, off_z, off_x, jnp.where(same, 0.0, 1.0))
            amp = env * rinv
            damp = -(m * (1.0 / 9.0) + env * (rinv * rinv))
            amp_r = amp * rinv
            amp_c = amp * (np.pi / CUTOFF)
            for c in range(3):
                uu_[n, c, rows, :] = u[c]
            two_c = 2.0 * c1
            s_prev, s_now = jnp.zeros_like(s1), s1
            c_prev, c_now = jnp.ones_like(c1), c1
            for k in range(K):
                lanes = slice(k * T, (k + 1) * T)
                e = s_now * amp
                pv[n, rows, lanes] = e.astype(BF16)
                for c in range(3):
                    pv[n, pl.ds((c + 1) * T + i0, IC), lanes] = (e * u[c]).astype(BF16)
                wk[n, k, rows, :] = s_now * amp_r
                dk[n, k, rows, :] = (c_now * float(k + 1)) * amp_c + s_now * damp
                s_prev, s_now = s_now, two_c * s_now - s_prev
                c_prev, c_now = c_now, two_c * c_now - c_prev
            return 0

        lax.fori_loop(0, T // IC, chunk, 0)

    pairs(jnp.int32(4))

    pl.semaphore_wait(bar, 4 + G - 1 + S - 1)

    def neighbour_copies(src, dst, send_sem, recv_sem, same_src):
        out = []
        for n, (dz, dx) in enumerate(OFFSETS):
            if n != 4:
                out.append(pltpu.make_async_remote_copy(
                    src_ref=src.at[4 if same_src else n], dst_ref=dst.at[8 - n],
                    send_sem=send_sem.at[n], recv_sem=recv_sem.at[8 - n],
                    device_id=peer(dz, dx), device_id_type=MESH))
        return out

    pos_copies = neighbour_copies(hpos, hpos, ps, pr_, True)
    for cp in pos_copies:
        cp.start()

    def sig_phase(k, _):
        pl.semaphore_signal(phase, inc=1, device_id=(g, lax.rem(s + k, S)), device_id_type=MESH)
        return 0

    lax.fori_loop(1, S, sig_phase, 0)
    pl.semaphore_wait(phase, S - 1)

    def exchange(src, dst, send_sem, recv_sem):
        own = pltpu.make_async_copy(src.at[me], dst.at[me], ls)
        own.start()

        def send(k, _):
            q = lax.rem(me + k, N)
            pltpu.make_async_remote_copy(
                src_ref=src.at[q], dst_ref=dst.at[me], send_sem=send_sem, recv_sem=recv_sem,
                device_id=(q // S, lax.rem(q, S)), device_id_type=MESH).start()
            return 0

        lax.fori_loop(1, N, send, 0)
        own.wait()

    def arrived(dst, sem):
        pltpu.make_async_copy(dst.at[pl.ds(0, N - 1)], dst.at[pl.ds(0, N - 1)], sem).wait()

    exchange(spec, plane, as_, ar)
    halo_copies = neighbour_copies(halo, halo, hs, hr, True)
    for cp in halo_copies:
        cp.start()

    for cp in pos_copies:
        cp.wait_recv()

    def pair_step(q, _):
        pairs(q + (q >= 4).astype(jnp.int32))
        return 0

    lax.fori_loop(0, 8, pair_step, 0)

    for t in loads[8:]:
        t.wait()
    arrived(plane, ar)
    rs = split(jnp.concatenate([plane[:, 0, :], plane[:, 1, :]], axis=1))
    yr = dot3((w[0, 0:N], w[1, 0:N]), rs, NN)
    yi = dot3((w[0, N:], w[1, N:]), rs, NN)
    tr, ti = tw[0], tw[1]
    yy = split(jnp.concatenate([tr * yr - ti * yi, tr * yi + ti * yr], axis=1))
    zz = dot3(yy, (fm[0], fm[1]), NN)
    zs = split(zz * jnp.concatenate([grn[...], grn[...]], axis=1))
    vv = dot3(zs, (fm[0], fm[1]), NT)
    vr, vi = vv[:, :ABP], vv[:, ABP:]
    p_r = split(tr * vr + ti * vi)
    p_i = split(tr * vi - ti * vr)
    uu = dot3((w[0, 0:N], w[1, 0:N]), p_r, NN) + dot3((w[0, N:], w[1, N:]), p_i, NN)
    back[:, 0, :] = uu[:, :128]
    back[:, 1, :] = uu[:, 128:]
    exchange(back, field, bs, br)

    for cp in halo_copies:
        cp.wait_recv()
    msg[...] = jnp.zeros_like(msg)

    def forward(n, _):
        feat = halo[n]
        for k in range(K):
            radt[n, k * T:(k + 1) * T, :] = (feat * rw_ref[k:k + 1, :]).astype(BF16)
        msg[...] += dg(pv[n], radt[n], NN)
        return 0

    lax.fori_loop(0, 9, forward, 0)

    m0 = msg[0:T]
    mc = [msg[(c + 1) * T:(c + 2) * T] for c in range(3)]
    inv = (m0 + (mc[0] * mc[0] + mc[1] * mc[1] + mc[2] * mc[2])).astype(BF16)
    mix = mix_ref[...]
    pre = dg(inv, mix, NN)
    sig = 1.0 / (1.0 + jnp.exp(-pre))
    owr = ow_ref[...]
    energy_col = jnp.sum(pre * sig * owr, axis=1, keepdims=True)
    energy_sr = jnp.transpose(jnp.broadcast_to(energy_col, (T, T)))[0:1, :]
    valid_col = jnp.transpose(jnp.broadcast_to(valid, (8, T)))[:, 0:1]
    grad_pre = ((sig + pre * sig * (1.0 - sig)) * owr * valid_col).astype(BF16)
    grad_inv = dg(grad_pre, mix, NT)
    gm[0:T] = grad_inv.astype(BF16)
    for c in range(3):
        gm[(c + 1) * T:(c + 2) * T] = (2.0 * mc[c] * grad_inv).astype(BF16)

    own_acc[...] = jnp.zeros_like(own_acc)

    def grad_dot(n, gp):
        gp[...] = dg(gm[...], radt[n], NT)

    def grad_pairs(n, gp):
        near = [None] * 3
        for t in range(T // 8):
            rows = slice(t * 8, (t + 1) * 8)
            tc = [None] * 3
            bb = [None] * 4
            for k in range(K):
                lanes = slice(k * T, (k + 1) * T)
                wv, dv = wk[n, k, rows, :], dk[n, k, rows, :]
                for c in range(4):
                    v = gp[c * T + t * 8:c * T + (t + 1) * 8, lanes]
                    bb[c] = v * dv if k == 0 else bb[c] + v * dv
                    if c:
                        tc[c - 1] = v * wv if k == 0 else tc[c - 1] + v * wv
            u = [uu_[n, c, rows, :] for c in range(3)]
            b = bb[0]
            for c in range(3):
                b = b + u[c] * (bb[c + 1] - tc[c])
            for c in range(3):
                gr = tc[c] + u[c] * b
                own_acc[c, rows, :] += gr
                near[c] = gr if t == 0 else near[c] + gr
        for c in range(3):
            ff[n, c:c + 1, :] = -jnp.sum(near[c], axis=0, keepdims=True)

    ff[...] = jnp.zeros_like(ff)
    grad_dot(0, gp_a)

    def backward(t, _):
        grad_dot(2 * t + 1, gp_b)
        grad_pairs(2 * t, gp_a)
        grad_dot(2 * t + 2, gp_a)
        grad_pairs(2 * t + 1, gp_b)
        return 0

    lax.fori_loop(0, 4, backward, 0)
    grad_pairs(8, gp_a)

    force_copies = neighbour_copies(ff, fr, fs, fr_sem, False)
    for cp in force_copies:
        cp.start()

    arrived(field, br)
    phi = split(jnp.concatenate([field[:, 0, :], field[:, 1, :]], axis=1))
    along = dot3(phi, (ee[0], ee[1]), TN)
    a_w, a_s = along[:, :T], along[:, T:]
    pot = jnp.sum(a_w * wzx[0], axis=0, keepdims=True)
    rec = [
        -charge * jnp.sum(a_w * wzx[1], axis=0, keepdims=True),
        -charge * jnp.sum(a_w * wzx[2], axis=0, keepdims=True),
        -charge * jnp.sum(a_s * wzx[0], axis=0, keepdims=True),
    ]
    e_out[...] = valid * (energy_sr + 0.5 * charge * pot)
    own_rows = []
    for c in range(3):
        col = jnp.sum(own_acc[c], axis=1, keepdims=True)
        own_rows.append(jnp.transpose(jnp.broadcast_to(col, (T, T)))[0:1, :])

    for cp in force_copies:
        cp.wait_recv()
    near = ff[4]
    for n in range(9):
        if n != 4:
            near = near + fr[n]
    for c in range(3):
        f_out[c] = own_rows[c] + near[c:c + 1, :] + rec[c]
    for cp in pos_copies + halo_copies + force_copies:
        cp.wait_send()
    arrived(spec, as_)
    arrived(back, bs)


def local(G, S, positions, features, cell_counts, radial_weights, mix_weights, out_weights,
          charge_weights, spline_base, spline_weights, spline_slopes):
    N = G * S
    hbm = pl.BlockSpec(memory_space=pltpu.HBM)
    vm = pl.BlockSpec(memory_space=pltpu.VMEM)
    V = pltpu.VMEM
    DMA = pltpu.SemaphoreType.DMA
    e, f = pl.pallas_call(
        functools.partial(kernel, G, S),
        out_shape=(jax.ShapeDtypeStruct((1, T), F32), jax.ShapeDtypeStruct((3, 1, T), F32)),
        in_specs=[hbm] * 14,
        out_specs=[vm, vm],
        scratch_shapes=[
            V((3, 1, T), F32), V((F, T), BF16), V((1, 1), jnp.int32), V((K, F), F32), V((F, F), BF16),
            V((1, F), F32), V((1, F), F32), V((3, 1, T), jnp.int32), V((12, 1, T), F32), V((12, 1, T), F32),
            V((2, N, N), BF16), V((2, 2 * N, N), BF16), V((2, N, ABP), F32), V((2, 2 * ABP, 256), BF16),
            V((9, T, F), F32), V((9, 8, T), F32), V((3, T, T), F32), V((9, 4 * T, K * T), BF16),
            V((9, K, T, T), F32), V((9, K, T, T), F32), V((9, 3, T, T), F32), V((9, K * T, F), BF16),
            V((4 * T, F), F32), V((4 * T, F), BF16), V((4 * T, K * T), F32), V((4 * T, K * T), F32),
            V((3, T, T), F32), V((9, 8, T), F32), V((9, 8, T), F32),
            V((2, N, 2 * T), BF16), V((3, ABP, T), F32),
            V((N, 2, 128), F32), V((N, 2, 128), F32), V((N, 2, 128), F32), V((N, 2, 128), F32),
            V((N, 128), F32),
            DMA((14,)), DMA((9,)), DMA((9,)), DMA((9,)), DMA((9,)), DMA((9,)), DMA((9,)),
            DMA, DMA, DMA, DMA, DMA, pltpu.SemaphoreType.REGULAR,
        ],
        compiler_params=pltpu.CompilerParams(collective_id=0, has_side_effects=True,
                                             vmem_limit_bytes=60 * 1024 * 1024),
    )(
        positions.reshape(3, 1, T), features.reshape(F, T), cell_counts, radial_weights, mix_weights,
        out_weights.reshape(1, F), charge_weights.reshape(1, F), spline_base.reshape(3, 1, T),
        spline_weights.reshape(12, 1, T), spline_slopes.reshape(12, 1, T),
        *[jnp.asarray(t) for t in tables(G, S)],
    )
    return e.reshape(1, 1, T), f.reshape(3, 1, 1, T)


def solution(mesh):
    placed = (
        P(None, "gz", "xy", None), P(None, "gz", "xy", None), P("gz", "xy"), P(), P(), P(), P(),
        P(None, "gz", "xy", None), P(None, None, "gz", "xy", None), P(None, None, "gz", "xy", None),
    )
    return jax.shard_map(
        functools.partial(local, mesh.shape["gz"], mesh.shape["xy"]),
        mesh=mesh, in_specs=placed,
        out_specs=(P("gz", "xy", None), P(None, "gz", "xy", None)),
        check_vma=False,
    )
```

time: 71 us -> 52.8 us (0.74)
  Pallas kernels: 62.1 us -> 49.7 us
  local copies, waits for them, and re-layouts: 7.13 us -> 1.69 us
    pallas_call x1, Pallas kernels: 62.1 us -> 49.7 us  [local(): pl.pallas_call(functools.partial(kernel, G, S), out_shape=(jax.ShapeDtype...]
    unnamed x32 -> x6, local copies, waits for them, and re-layouts: 7.13 us -> 1.69 us
where the time goes in v1:
time: 52.8 us; the launch traced here: 52.7 us
  Pallas kernels  49.7 us (94%)
  local copies, waits for them, and re-layouts  1.69 us (3%)
  between operations  1.3 us (2%)
    pallas_call x1, Pallas kernels, local(): pl.pallas_call(functools.partial(kernel, G, S), out_shape=(jax.ShapeDtype...  49.7 us
    unnamed x6, local copies, waits for them, and re-layouts  1.69 us

profile of v1, /device:TPU:1, one launch (start us, length us, event | category | flops | bytes accessed | tf_op | source)
XLA Modules:
  0.0 52.7 jit_solution(370278230231569777)
XLA Ops:
  1.3 49.7 %shard_map.149 = (f32[1,128]{1,0:T(1,128)}, f32[3,1,128]{2,1,0:T(1,128)}) custom-call(f32[3,1,128]{2,1,0:T(1,128)} %bitcast.14, bf16[128,128]{1,0:T(8,128)(2,1)} %bitcast.11, s32[1,1]{1,0:T(1,128)S(6)} %copy.19.cnt_hbm, f32[8,128]{1,0:T(8,128)} %rw_hbm.1, bf16[128,128]{1,0:T(8,128)(2,1)} %mix_hbm.1, f32[1,128]{1,0:T(1,128)} %bitcast.17, f32[1,128]{1,0:T(1,128)} %bitcast.18, ...), custom_call_target="tpu_custom_call" | custom-call | tf_op jit(solution)/shard_map/pallas_call | solution.py:451
  50.9 0.0 copy-start.1
  51.0 0.0 copy-start
  51.0 0.6 %copy-done.1 = f32[1,128]{1,0:T(1,128)S(1)} copy-done((f32[1,128]{1,0:T(1,128)S(1)}, f32[1,128]{1,0:T(1,128)}, u32[]{:S(2)}) %copy-start.1) | copy-done | bytes 536
  51.6 0.5 copy.20
  52.1 0.0 copy-done
  52.1 0.6 %copy.21 = f32[3,1,1,128]{3,2,1,0:T(1,128)} copy(f32[3,1,1,128]{3,2,1,0:T(1,128)S(1)} %bitcast.16) | data formatting | bytes 3072
Async XLA Ops:
  50.9 0.6 %copy-start.1 = (f32[1,128]{1,0:T(1,128)S(1)}, f32[1,128]{1,0:T(1,128)}, u32[]{:S(2)}) copy-start(f32[1,128]{1,0:T(1,128)} %get-tuple-element.4) | copy-start | bytes 1540
  51.0 1.1 %copy-start = (f32[3,1,128]{2,1,0:T(1,128)S(1)}, f32[3,1,128]{2,1,0:T(1,128)}, u32[]{:S(2)}) copy-start(f32[3,1,128]{2,1,0:T(1,128)} %get-tuple-element.5) | copy-start | bytes 4612

commit v2 on v1

--- a/solution.py
+++ b/solution.py
@@ -37,6 +37,10 @@
     return np.stack([hi, lo])
 
 
+def half_rows(N):
+    return -(-(N // 2 + 2) // 16) * 16
+
+
 @functools.lru_cache(None)
 def tables(G, S):
     MZ, MX, MY, N = G * BZ, S * BX, G * S, G * S
@@ -46,11 +50,19 @@
     ct = np.where((p <= MY // 2)[:, None], np.cos(ang), np.sin(ang))
     kzl = np.repeat(np.arange(G), S)
     kxl = np.tile(np.arange(S), G)
-    ang = 2 * np.pi * (((kzl[:, None] * kzl[None, :]) % G) / G + ((kxl[:, None] * kxl[None, :]) % S) / S)
+    mate = (-kzl % G) * S + (-kxl % S)
+    rows = np.arange(N)
+    kept = rows[rows <= mate]
+    count = np.where(kept == mate[kept], 1.0, 2.0)
+    fill = half_rows(N) - len(kept)
+    kept = np.concatenate([kept, np.zeros(fill, np.int64)])
+    count = np.concatenate([count, np.zeros(fill)])
+    rz, rx = kzl[kept], kxl[kept]
+    ang = 2 * np.pi * (((rz[:, None] * kzl[None, :]) % G) / G + ((rx[:, None] * kxl[None, :]) % S) / S)
     w = np.concatenate([np.cos(ang), -np.sin(ang)], axis=0)
     a = np.repeat(np.arange(EZ), EX)
     b = np.tile(np.arange(EX), EZ)
-    ang = 2 * np.pi * (kzl[:, None] * (a - 1)[None] / MZ + kxl[:, None] * (b - 1)[None] / MX)
+    ang = 2 * np.pi * (rz[:, None] * (a - 1)[None] / MZ + rx[:, None] * (b - 1)[None] / MX)
     pad = ((0, 0), (0, ABP - EZ * EX))
     tw = np.stack([np.pad(np.cos(ang), pad), np.pad(-np.sin(ang), pad)]).astype(np.float32)
     kzh = np.repeat(np.arange(BZ), BX)
@@ -59,7 +71,14 @@
     pad = ((0, ABP - EZ * EX), (0, 0))
     mr, mi = np.pad(np.cos(ang), pad), np.pad(-np.sin(ang), pad)
     fm = np.block([[mr, mi], [-mi, mr]])
-    return split_np(ct), split_np(w), tw, split_np(fm)
+    kz = rz[:, None] + G * kzh[None]
+    kx = rx[:, None] + S * kxh[None]
+    kz = kz - MZ * (2 * kz >= MZ)
+    kx = kx - MX * (2 * kx >= MX)
+    wave = (kz / (EDGE_LEN * G)) ** 2 + (kx / (EDGE_LEN * S)) ** 2
+    scale = np.broadcast_to(count[:, None], wave.shape)
+    gr = np.stack([wave, scale]).astype(np.float32)
+    return split_np(ct), split_np(w), split_np(w.T), tw, split_np(fm), gr
 
 
 def fit(fn, degree, top):
@@ -118,10 +137,10 @@
 def kernel(
     G, S,
     pos_hbm, feat_hbm, cnt_hbm, rw_hbm, mix_hbm, ow_hbm, cw_hbm, base_hbm, wts_hbm, slp_hbm,
-    ct_hbm, w_hbm, tw_hbm, fm_hbm,
+    ct_hbm, w_hbm, wt_hbm, tw_hbm, fm_hbm, gr_hbm,
     e_out, f_out,
     pos_ref, feat_ref, cnt_ref, rw_ref, mix_ref, ow_ref, cw_ref, base_ref, wts_ref, slp_ref,
-    ct, w, tw, fm,
+    ct, w, wt, tw, fm, gr,
     halo, hpos, posb, pv, wk, dk, uu_, radt, msg, gm, gp_a, gp_b, own_acc, ff, fr,
     ee, wzx, spec, plane, back, field, grn,
     in_sem, hs, hr, ps, pr_, fs, fr_sem, as_, ar, bs, br, ls, phase,
@@ -139,7 +158,7 @@
         (feat_hbm, feat_ref), (cnt_hbm, cnt_ref), (cw_hbm, cw_ref), (base_hbm, base_ref),
         (wts_hbm, wts_ref), (slp_hbm, slp_ref), (pos_hbm, pos_ref), (ct_hbm, ct),
         (rw_hbm, rw_ref), (mix_hbm, mix_ref), (ow_hbm, ow_ref),
-        (w_hbm, w), (tw_hbm, tw), (fm_hbm, fm)])]
+        (w_hbm, w), (wt_hbm, wt), (tw_hbm, tw), (fm_hbm, fm), (gr_hbm, gr)])]
     for t in loads:
         t.start()
 
@@ -169,56 +188,60 @@
     yrow = lax.broadcasted_iota(jnp.int32, (MY, T), 0)
     ty = jnp.bitwise_and(yrow - base_ref[2] + 1, MY - 1)
     wy = jnp.zeros((MY, T), F32)
-    sy = jnp.zeros((MY, T), F32)
     for c in range(4):
-        hit = ty == c
-        wy = wy + jnp.where(hit, wts_ref[8 + c], 0.0)
-        sy = sy + jnp.where(hit, slp_ref[8 + c], 0.0)
+        wy = wy + jnp.where(ty == c, wts_ref[8 + c], 0.0)
     ab = lax.broadcasted_iota(jnp.int32, (ABP, T), 0)
     arow = lax.shift_right_logical(ab * 373, 12)
     brow = ab - arow * EX
     tz = arow - (base_ref[0] - g * BZ)
     tx = brow - (base_ref[1] - s * BX)
     zero = jnp.zeros((ABP, T), F32)
-    wz, sz, wx, sx = zero, zero, zero, zero
+    wz, wx = zero, zero
     for c in range(4):
-        hit = tz == c
-        wz = wz + jnp.where(hit, wts_ref[c], 0.0)
-        sz = sz + jnp.where(hit, slp_ref[c], 0.0)
-        hit = tx == c
-        wx = wx + jnp.where(hit, wts_ref[4 + c], 0.0)
-        sx = sx + jnp.where(hit, slp_ref[4 + c], 0.0)
+        wz = wz + jnp.where(tz == c, wts_ref[c], 0.0)
+        wx = wx + jnp.where(tx == c, wts_ref[4 + c], 0.0)
     wzx[0] = wz * wx
-    wzx[1] = sz * wx
-    wzx[2] = wz * sx
-
-    yw = split(jnp.concatenate([wy, sy], axis=1))
-    e_all = dot3((ct[0], ct[1]), yw, NN)
-    eh, el = split(e_all)
-    ee[0] = eh
-    ee[1] = el
-    spectrum = dot3((eh[:, :T], el[:, :T]), split(wzx[0] * charge), NT)
+
+    eh, el = split(dot3((ct[0], ct[1]), split(wy), NN))
+    ee[0, :, :T] = eh
+    ee[1, :, :T] = el
+    spectrum = dot3((eh, el), split(wz * wx * charge), NT)
     spec[:, 0, :] = spectrum[:, :128]
     spec[:, 1, :] = spectrum[:, 128:]
 
-    kk = lax.broadcasted_iota(jnp.int32, (N, 128), 0)
-    hh = lax.broadcasted_iota(jnp.int32, (N, 128), 1)
-    kz = kk // S + G * (hh // BX)
-    kx = lax.rem(kk, S) + S * lax.rem(hh, BX)
-    mz_, mx_ = G * BZ, S * BX
-    kz = (kz - mz_ * (2 * kz >= mz_).astype(jnp.int32)).astype(F32)
-    kx = (kx - mx_ * (2 * kx >= mx_).astype(jnp.int32)).astype(F32)
-    ky = jnp.where(me <= MY // 2, me, me - MY // 2).astype(F32)
-    twice = jnp.where(jnp.logical_or(me == 0, me == MY // 2), 1.0, 2.0)
-    len_z, len_x = EDGE_LEN * G, EDGE_LEN * S
-    fz, fx, fy = kz * (1.0 / len_z), kx * (1.0 / len_x), ky * (1.0 / PERIOD_Y)
-    wsq = fz * fz + fx * fx + fy * fy
-    positive = wsq > 0
-    safe = jnp.where(positive, wsq, 1.0)
-    green = COULOMB * jnp.exp(safe * (-np.pi ** 2 / EWALD_BETA ** 2)) / (
-        np.pi * len_z * len_x * PERIOD_Y * safe)
-    grn[...] = jnp.where(positive, green * twice, 0.0)
-
+    pl.semaphore_wait(bar, 4 + G - 1 + S - 1)
+
+    def neighbour_copies(src, dst, send_sem, recv_sem, same_src):
+        out = []
+        for n, (dz, dx) in enumerate(OFFSETS):
+            if n != 4:
+                out.append(pltpu.make_async_remote_copy(
+                    src_ref=src.at[4 if same_src else n], dst_ref=dst.at[8 - n],
+                    send_sem=send_sem.at[n], recv_sem=recv_sem.at[8 - n],
+                    device_id=peer(dz, dx), device_id_type=MESH))
+        return out
+
+    pos_copies = neighbour_copies(hpos, hpos, ps, pr_, True)
+    for cp in pos_copies:
+        cp.start()
+
+    def feature_copy(src, dst, dz, dx):
+        return pltpu.make_async_remote_copy(
+            src_ref=halo.at[src], dst_ref=halo.at[dst], send_sem=hs.at[dst], recv_sem=hr.at[dst],
+            device_id=peer(dz, dx), device_id_type=MESH)
+
+    side_z = [feature_copy(4, 1, 1, 0), feature_copy(4, 7, -1, 0)]
+    side_x = [feature_copy(4, 3, 0, 1), feature_copy(4, 5, 0, -1)]
+    corners = [feature_copy(1, 0, 0, 1), feature_copy(1, 2, 0, -1),
+               feature_copy(7, 6, 0, 1), feature_copy(7, 8, 0, -1)]
+    for cp in side_z + side_x:
+        cp.start()
+
+    def sig_phase(k, _):
+        pl.semaphore_signal(phase, inc=1, device_id=(g, lax.rem(s + k, S)), device_id_type=MESH)
+        return 0
+
+    lax.fori_loop(1, S, sig_phase, 0)
     own_t = jnp.transpose(hpos[4])
     for c in range(3):
         posb[c] = jnp.broadcast_to(own_t[:, c:c + 1], (T, T))
@@ -262,50 +285,64 @@
 
     pairs(jnp.int32(4))
 
-    pl.semaphore_wait(bar, 4 + G - 1 + S - 1)
-
-    def neighbour_copies(src, dst, send_sem, recv_sem, same_src):
-        out = []
-        for n, (dz, dx) in enumerate(OFFSETS):
-            if n != 4:
-                out.append(pltpu.make_async_remote_copy(
-                    src_ref=src.at[4 if same_src else n], dst_ref=dst.at[8 - n],
-                    send_sem=send_sem.at[n], recv_sem=recv_sem.at[8 - n],
-                    device_id=peer(dz, dx), device_id_type=MESH))
-        return out
-
-    pos_copies = neighbour_copies(hpos, hpos, ps, pr_, True)
-    for cp in pos_copies:
-        cp.start()
-
-    def sig_phase(k, _):
-        pl.semaphore_signal(phase, inc=1, device_id=(g, lax.rem(s + k, S)), device_id_type=MESH)
-        return 0
-
-    lax.fori_loop(1, S, sig_phase, 0)
     pl.semaphore_wait(phase, S - 1)
 
     def exchange(src, dst, send_sem, recv_sem):
         own = pltpu.make_async_copy(src.at[me], dst.at[me], ls)
         own.start()
 
-        def send(k, _):
-            q = lax.rem(me + k, N)
+        def one(j, dz):
+            x2 = lax.bitwise_and((g // 2) + lax.bitwise_and(lax.shift_right_logical(0x36, 2 * (j // 8)), 3), 3)
+            dy = lax.bitwise_and(lax.shift_right_logical(0x36, 2 * lax.rem(j // 2, 4)), 3)
+            y2 = lax.bitwise_and(2 * lax.rem(g, 2) + lax.rem(s // 2, 2) + dy, 3)
+            z2 = lax.bitwise_and(s // 4 + dz, 7)
+            gq = 2 * x2 + y2 // 2
+            sq = 4 * z2 + 2 * lax.rem(y2, 2) + lax.rem(s + j + 1, 2)
             pltpu.make_async_remote_copy(
-                src_ref=src.at[q], dst_ref=dst.at[me], send_sem=send_sem, recv_sem=recv_sem,
-                device_id=(q // S, lax.rem(q, S)), device_id_type=MESH).start()
+                src_ref=src.at[gq * S + sq], dst_ref=dst.at[me], send_sem=send_sem, recv_sem=recv_sem,
+                device_id=(gq, sq), device_id_type=MESH).start()
+
+        def send(j, _):
+            for dz in (4, 5, 3, 6, 2, 7, 1, 0):
+                one(j, dz)
             return 0
 
-        lax.fori_loop(1, N, send, 0)
+        lax.fori_loop(0, 31, send, 0)
+        for dz in (4, 5, 3, 6, 2, 7, 1):
+            one(jnp.int32(31), dz)
         own.wait()
 
     def arrived(dst, sem):
         pltpu.make_async_copy(dst.at[pl.ds(0, N - 1)], dst.at[pl.ds(0, N - 1)], sem).wait()
 
     exchange(spec, plane, as_, ar)
-    halo_copies = neighbour_copies(halo, halo, hs, hr, True)
-    for cp in halo_copies:
-        cp.start()
+
+    sy = jnp.zeros((MY, T), F32)
+    for c in range(4):
+        sy = sy + jnp.where(ty == c, slp_ref[8 + c], 0.0)
+    eh, el = split(dot3((ct[0], ct[1]), split(sy), NN))
+    ee[0, :, T:] = eh
+    ee[1, :, T:] = el
+    wz, sz, wx, sx = zero, zero, zero, zero
+    for c in range(4):
+        hit = tz == c
+        wz = wz + jnp.where(hit, wts_ref[c], 0.0)
+        sz = sz + jnp.where(hit, slp_ref[c], 0.0)
+        hit = tx == c
+        wx = wx + jnp.where(hit, wts_ref[4 + c], 0.0)
+        sx = sx + jnp.where(hit, slp_ref[4 + c], 0.0)
+    wzx[1] = sz * wx
+    wzx[2] = wz * sx
+    for t in loads[8:]:
+        t.wait()
+    ky = jnp.where(me <= MY // 2, me, me - MY // 2).astype(F32) * (1.0 / PERIOD_Y)
+    twice = jnp.where(jnp.logical_or(me == 0, me == MY // 2), 1.0, 2.0)
+    wsq = gr[0] + ky * ky
+    positive = wsq > 0
+    safe = jnp.where(positive, wsq, 1.0)
+    green = COULOMB * jnp.exp(safe * (-np.pi ** 2 / EWALD_BETA ** 2)) / (
+        (np.pi * EDGE_LEN * G * EDGE_LEN * S * PERIOD_Y) * safe)
+    grn[...] = jnp.where(positive, green * twice, 0.0) * gr[1]
 
     for cp in pos_copies:
         cp.wait_recv()
@@ -314,39 +351,47 @@
         pairs(q + (q >= 4).astype(jnp.int32))
         return 0
 
-    lax.fori_loop(0, 8, pair_step, 0)
-
-    for t in loads[8:]:
-        t.wait()
+    lax.fori_loop(0, 4, pair_step, 0)
+    for cp in side_z:
+        cp.wait_recv()
+    for cp in corners:
+        cp.start()
+    lax.fori_loop(4, 8, pair_step, 0)
+
+    msg[...] = jnp.zeros_like(msg)
+
+    def forward(n):
+        feat = halo[n]
+        for k in range(K):
+            radt[n, k * T:(k + 1) * T, :] = (feat * rw_ref[k:k + 1, :]).astype(BF16)
+        msg[...] += dg(pv[n], radt[n], NN)
+        return 0
+
+    for cp in side_x:
+        cp.wait_recv()
+    forward(4)
+    lax.fori_loop(0, 4, lambda q, _: forward(2 * q + 1), 0)
+
     arrived(plane, ar)
     rs = split(jnp.concatenate([plane[:, 0, :], plane[:, 1, :]], axis=1))
-    yr = dot3((w[0, 0:N], w[1, 0:N]), rs, NN)
-    yi = dot3((w[0, N:], w[1, N:]), rs, NN)
+    y_all = dot3((w[0], w[1]), rs, NN)
+    H = half_rows(N)
+    yr, yi = y_all[:H], y_all[H:]
     tr, ti = tw[0], tw[1]
     yy = split(jnp.concatenate([tr * yr - ti * yi, tr * yi + ti * yr], axis=1))
     zz = dot3(yy, (fm[0], fm[1]), NN)
     zs = split(zz * jnp.concatenate([grn[...], grn[...]], axis=1))
     vv = dot3(zs, (fm[0], fm[1]), NT)
     vr, vi = vv[:, :ABP], vv[:, ABP:]
-    p_r = split(tr * vr + ti * vi)
-    p_i = split(tr * vi - ti * vr)
-    uu = dot3((w[0, 0:N], w[1, 0:N]), p_r, NN) + dot3((w[0, N:], w[1, N:]), p_i, NN)
+    vs = split(jnp.concatenate([tr * vr + ti * vi, tr * vi - ti * vr], axis=0))
+    uu = dot3((wt[0], wt[1]), vs, NN)
     back[:, 0, :] = uu[:, :128]
     back[:, 1, :] = uu[:, 128:]
     exchange(back, field, bs, br)
 
-    for cp in halo_copies:
+    for cp in corners:
         cp.wait_recv()
-    msg[...] = jnp.zeros_like(msg)
-
-    def forward(n, _):
-        feat = halo[n]
-        for k in range(K):
-            radt[n, k * T:(k + 1) * T, :] = (feat * rw_ref[k:k + 1, :]).astype(BF16)
-        msg[...] += dg(pv[n], radt[n], NN)
-        return 0
-
-    lax.fori_loop(0, 9, forward, 0)
+    lax.fori_loop(0, 4, lambda q, _: forward(2 * q + 2 * (q >= 2).astype(jnp.int32)), 0)
 
     m0 = msg[0:T]
     mc = [msg[(c + 1) * T:(c + 2) * T] for c in range(3)]
@@ -435,7 +480,7 @@
             near = near + fr[n]
     for c in range(3):
         f_out[c] = own_rows[c] + near[c:c + 1, :] + rec[c]
-    for cp in pos_copies + halo_copies + force_copies:
+    for cp in pos_copies + side_z + side_x + corners + force_copies:
         cp.wait_send()
     arrived(spec, as_)
     arrived(back, bs)
@@ -444,6 +489,7 @@
 def local(G, S, positions, features, cell_counts, radial_weights, mix_weights, out_weights,
           charge_weights, spline_base, spline_weights, spline_slopes):
     N = G * S
+    H = half_rows(N)
     hbm = pl.BlockSpec(memory_space=pltpu.HBM)
     vm = pl.BlockSpec(memory_space=pltpu.VMEM)
     V = pltpu.VMEM
@@ -451,20 +497,21 @@
     e, f = pl.pallas_call(
         functools.partial(kernel, G, S),
         out_shape=(jax.ShapeDtypeStruct((1, T), F32), jax.ShapeDtypeStruct((3, 1, T), F32)),
-        in_specs=[hbm] * 14,
+        in_specs=[hbm] * 16,
         out_specs=[vm, vm],
         scratch_shapes=[
             V((3, 1, T), F32), V((F, T), BF16), V((1, 1), jnp.int32), V((K, F), F32), V((F, F), BF16),
             V((1, F), F32), V((1, F), F32), V((3, 1, T), jnp.int32), V((12, 1, T), F32), V((12, 1, T), F32),
-            V((2, N, N), BF16), V((2, 2 * N, N), BF16), V((2, N, ABP), F32), V((2, 2 * ABP, 256), BF16),
+            V((2, N, N), BF16), V((2, 2 * H, N), BF16), V((2, N, 2 * H), BF16), V((2, H, ABP), F32), V((2, 2 * ABP, 256), BF16),
+            V((2, H, 128), F32),
             V((9, T, F), F32), V((9, 8, T), F32), V((3, T, T), F32), V((9, 4 * T, K * T), BF16),
             V((9, K, T, T), F32), V((9, K, T, T), F32), V((9, 3, T, T), F32), V((9, K * T, F), BF16),
             V((4 * T, F), F32), V((4 * T, F), BF16), V((4 * T, K * T), F32), V((4 * T, K * T), F32),
             V((3, T, T), F32), V((9, 8, T), F32), V((9, 8, T), F32),
             V((2, N, 2 * T), BF16), V((3, ABP, T), F32),
             V((N, 2, 128), F32), V((N, 2, 128), F32), V((N, 2, 128), F32), V((N, 2, 128), F32),
-            V((N, 128), F32),
-            DMA((14,)), DMA((9,)), DMA((9,)), DMA((9,)), DMA((9,)), DMA((9,)), DMA((9,)),
+            V((H, 128), F32),
+            DMA((16,)), DMA((9,)), DMA((9,)), DMA((9,)), DMA((9,)), DMA((9,)), DMA((9,)),
             DMA, DMA, DMA, DMA, DMA, pltpu.SemaphoreType.REGULAR,
         ],
         compiler_params=pltpu.CompilerParams(collective_id=0, has_side_effects=True,

time: 52.8 us -> 45.7 us (0.87)
  Pallas kernels: 49.7 us -> 42.6 us
    pallas_call x1, Pallas kernels: 49.7 us -> 42.6 us  [local(): pl.pallas_call(functools.partial(kernel, G, S), out_shape=(jax.ShapeDtype...]
where the time goes in v2:
time: 45.7 us; the launch traced here: 45.6 us
  Pallas kernels  42.6 us (93%)
  local copies, waits for them, and re-layouts  1.69 us (4%)
  between operations  1.3 us (3%)
    pallas_call x1, Pallas kernels, local(): pl.pallas_call(functools.partial(kernel, G, S), out_shape=(jax.ShapeDtype...  42.6 us
    unnamed x6, local copies, waits for them, and re-layouts  1.69 us

profile of v2, /device:TPU:1, one launch (start us, length us, event | category | flops | bytes accessed | tf_op | source)
XLA Modules:
  0.0 45.6 jit_solution(1309992623996659544)
XLA Ops:
  1.3 42.6 %shard_map.167 = (f32[1,128]{1,0:T(1,128)}, f32[3,1,128]{2,1,0:T(1,128)}) custom-call(f32[3,1,128]{2,1,0:T(1,128)} %bitcast.14, bf16[128,128]{1,0:T(8,128)(2,1)} %bitcast.11, s32[1,1]{1,0:T(1,128)S(6)} %copy.21.cnt_hbm, f32[8,128]{1,0:T(8,128)} %rw_hbm.1, bf16[128,128]{1,0:T(8,128)(2,1)} %mix_hbm.1, f32[1,128]{1,0:T(1,128)} %bitcast.17, f32[1,128]{1,0:T(1,128)} %bitcast.18, ...), custom_call_target="tpu_custom_call" | custom-call | tf_op jit(solution)/shard_map/pallas_call | solution.py:497
  43.9 0.0 copy-start.1
  43.9 0.0 copy-start
  43.9 0.6 %copy-done.1 = f32[1,128]{1,0:T(1,128)S(1)} copy-done((f32[1,128]{1,0:T(1,128)S(1)}, f32[1,128]{1,0:T(1,128)}, u32[]{:S(2)}) %copy-start.1) | copy-done | bytes 536
  44.5 0.5 %copy.22 = f32[1,1,128]{2,1,0:T(1,128)} copy(f32[1,1,128]{2,1,0:T(1,128)S(1)} %bitcast.19) | data formatting | bytes 1024
  45.0 0.0 copy-done
  45.0 0.6 %copy.23 = f32[3,1,1,128]{3,2,1,0:T(1,128)} copy(f32[3,1,1,128]{3,2,1,0:T(1,128)S(1)} %bitcast.16) | data formatting | bytes 3072
Async XLA Ops:
  43.9 0.6 %copy-start.1 = (f32[1,128]{1,0:T(1,128)S(1)}, f32[1,128]{1,0:T(1,128)}, u32[]{:S(2)}) copy-start(f32[1,128]{1,0:T(1,128)} %get-tuple-element.4) | copy-start | bytes 1540
  43.9 1.1 %copy-start = (f32[3,1,128]{2,1,0:T(1,128)S(1)}, f32[3,1,128]{2,1,0:T(1,128)}, u32[]{:S(2)}) copy-start(f32[3,1,128]{2,1,0:T(1,128)} %get-tuple-element.5) | copy-start | bytes 4612

commit v3 on v2

--- a/solution.py
+++ b/solution.py
@@ -442,19 +442,22 @@
     ff[...] = jnp.zeros_like(ff)
     grad_dot(0, gp_a)
 
+    def nth(q):
+        return jnp.where(q == 8, 4, q + (q >= 4).astype(jnp.int32))
+
     def backward(t, _):
-        grad_dot(2 * t + 1, gp_b)
-        grad_pairs(2 * t, gp_a)
-        grad_dot(2 * t + 2, gp_a)
-        grad_pairs(2 * t + 1, gp_b)
+        grad_dot(nth(2 * t + 1), gp_b)
+        grad_pairs(nth(2 * t), gp_a)
+        grad_dot(nth(2 * t + 2), gp_a)
+        grad_pairs(nth(2 * t + 1), gp_b)
         return 0
 
     lax.fori_loop(0, 4, backward, 0)
-    grad_pairs(8, gp_a)
 
     force_copies = neighbour_copies(ff, fr, fs, fr_sem, False)
     for cp in force_copies:
         cp.start()
+    grad_pairs(4, gp_a)
 
     arrived(field, br)
     phi = split(jnp.concatenate([field[:, 0, :], field[:, 1, :]], axis=1))

time: 45.7 us -> 45.4 us (level)
  no operation moved by 1% of the time
where the time goes in v3:
time: 45.4 us; the launch traced here: 45.3 us
  Pallas kernels  42.3 us (93%)
  local copies, waits for them, and re-layouts  1.69 us (4%)
  between operations  1.3 us (3%)
    pallas_call x1, Pallas kernels, local(): pl.pallas_call(functools.partial(kernel, G, S), out_shape=(jax.ShapeDtype...  42.3 us
    unnamed x6, local copies, waits for them, and re-layouts  1.69 us

profile of v3, /device:TPU:1, one launch (start us, length us, event | category | flops | bytes accessed | tf_op | source)
XLA Modules:
  0.0 45.3 jit_solution(16558159130419410803)
XLA Ops:
  1.3 42.3 %shard_map.167 = (f32[1,128]{1,0:T(1,128)}, f32[3,1,128]{2,1,0:T(1,128)}) custom-call(f32[3,1,128]{2,1,0:T(1,128)} %bitcast.14, bf16[128,128]{1,0:T(8,128)(2,1)} %bitcast.11, s32[1,1]{1,0:T(1,128)S(6)} %copy.21.cnt_hbm, f32[8,128]{1,0:T(8,128)} %rw_hbm.1, bf16[128,128]{1,0:T(8,128)(2,1)} %mix_hbm.1, f32[1,128]{1,0:T(1,128)} %bitcast.17, f32[1,128]{1,0:T(1,128)} %bitcast.18, ...), custom_call_target="tpu_custom_call" | custom-call | tf_op jit(solution)/shard_map/pallas_call | solution.py:500
  43.6 0.0 copy-start.1
  43.6 0.0 copy-start
  43.6 0.6 %copy-done.1 = f32[1,128]{1,0:T(1,128)S(1)} copy-done((f32[1,128]{1,0:T(1,128)S(1)}, f32[1,128]{1,0:T(1,128)}, u32[]{:S(2)}) %copy-start.1) | copy-done | bytes 536
  44.2 0.5 %copy.22 = f32[1,1,128]{2,1,0:T(1,128)} copy(f32[1,1,128]{2,1,0:T(1,128)S(1)} %bitcast.19) | data formatting | bytes 1024
  44.7 0.0 copy-done
  44.7 0.6 %copy.23 = f32[3,1,1,128]{3,2,1,0:T(1,128)} copy(f32[3,1,1,128]{3,2,1,0:T(1,128)S(1)} %bitcast.16) | data formatting | bytes 3072
Async XLA Ops:
  43.6 0.6 %copy-start.1 = (f32[1,128]{1,0:T(1,128)S(1)}, f32[1,128]{1,0:T(1,128)}, u32[]{:S(2)}) copy-start(f32[1,128]{1,0:T(1,128)} %get-tuple-element.4) | copy-start | bytes 1540
  43.6 1.1 %copy-start = (f32[3,1,128]{2,1,0:T(1,128)S(1)}, f32[3,1,128]{2,1,0:T(1,128)}, u32[]{:S(2)}) copy-start(f32[3,1,128]{2,1,0:T(1,128)} %get-tuple-element.5) | copy-start | bytes 4612
